TPU v7x, 512 devices: a whole 4x4x16 slice. The times are simulated.
512 devices in a mesh: off: 16 (over z_lo, y), img: 32 (over x, z_hi, core).
Axes of the slice: x: 4, y: 4, z: 16 (z_hi: 4, z_lo: 4; z = z_hi * 4 + z_lo), core: 2. Of those that a mesh axis runs over, the one named last changes fastest.
Arguments:
- traces: bfloat16 [16384, 3072], P(('off', 'img')), may hold values from -6 to 6
- offset_bins: int32 [16384], P(('off', 'img')), may hold values from 0 to 15, as said below
- class_slots: int32 [16384], P(('off', 'img')), may hold values from 0 to 1, as said below
- weights: bfloat16 [16, 16384, 1024], P('off', 'img'), may hold values from -0.1875 to 0.1875
- band_start: int32 [16, 128], P('off', 'img'), may hold values from 0 to 1536
- smoothing: int32 [16, 128], P('off', 'img'), may hold values from 0 to 1
Outputs:
- migrated: bfloat16 [16, 16384, 1536], P('off', 'img')
Inputs may be any that keep to these rules, and one draw needn't show every extreme that they name: `offset_bins`: in each aligned block of 32 traces every class is named by exactly 2 traces. Within each aligned block of 32 traces the pairs (offset_bins, class_slots) are all distinct.
All inputs are finite; a program needn't handle non-finite values.
Results may differ from a plain program's by a relative error of at most 0.005.
Values may be sent and summed in bfloat16 or wider, within the bound.
No kernel may reach another device: no remote copies, remote signals or barrier semaphores. Data moves between devices by JAX's collectives and lax.ppermute only.
A program may use at most 128 MiB of HBM per device.

v0:
```python
import jax
import jax.numpy as jnp
from jax import lax
from jax.sharding import PartitionSpec as P

NT = 1536
CB = 128


def filtered_levels(samples):
    values = samples.astype(jnp.float32)
    edges = [(0, 0)] * (values.ndim - 1)
    padded = jnp.pad(values, edges + [(1, 1)])
    boosted = values - 0.5 * (padded[..., :-2] + padded[..., 2:])
    widened = jnp.pad(boosted, edges + [(2, 2)])
    smoothed = (
        3.0 * boosted
        + 2.0 * (widened[..., 1:-3] + widened[..., 3:-1])
        + widened[..., :-4]
        + widened[..., 4:]
    ) / 9.0
    return jnp.stack([boosted, smoothed]).astype(jnp.bfloat16)


def migrate_rows(summed, shard_rows, weight_rows, band_rows, smooth_rows):
    row_count = shard_rows.shape[1]

    def segment(level_index, offset):
        return lax.dynamic_slice(shard_rows, (level_index, 0, offset), (1, row_count, NT))[0]

    segments = jax.vmap(segment)(smooth_rows, band_rows)
    blocks = band_rows.shape[0]
    columns = weight_rows
    columns = columns.reshape(blocks, CB, row_count)
    update = jnp.einsum("bcr,brt->bct", columns, segments, preferred_element_type=jnp.float32)
    return update.reshape(summed.shape)


def per_device(traces, offset_bins, class_slots, weights, band_start, smoothing):
    tr_count = traces.shape[0]
    per_class = tr_count // lax.axis_size("off")
    targets = offset_bins * per_class + class_slots
    weight_rows = weights[0]
    band_rows = band_start[0]
    smooth_rows = smoothing[0]
    initial = jnp.zeros((weight_rows.shape[0], NT), jnp.float32)
    levels = filtered_levels(traces)
    ordered = jnp.zeros_like(levels).at[:, targets].set(levels)
    regrouped = lax.all_to_all(ordered, "off", split_axis=1, concat_axis=1, tiled=True)
    summed = migrate_rows(
        initial,
        lax.all_gather(regrouped, "img", axis=1, tiled=True),
        weight_rows,
        band_rows,
        smooth_rows,
    )
    return summed.astype(jnp.bfloat16)[None]


def solution(mesh):
    in_specs = (
        P(("off", "img"), None),
        P(("off", "img")),
        P(("off", "img")),
        P("off", "img", None),
        P("off", "img"),
        P("off", "img"),
    )
    out_specs = P("off", "img", None)
    return jax.shard_map(
        per_device, mesh=mesh, in_specs=in_specs, out_specs=out_specs, check_vma=False
    )
```

profile of v0, /device:TPU:5, one launch (start us, length us, event | category | flops | bytes accessed | tf_op | source)
XLA Modules:
  0.0 268.0 jit_solution(2371842476114070729)
XLA Ops:
  6.5 0.0 all-gather.2.cloned.1.call-start
  6.5 1.0 convert_element_type.24
  7.6 0.3 convert_bitcast_fusion
  7.9 0.5 fusion.8
  8.4 0.4 copy.10
  8.8 0.7 compare_select_fusion.2
  9.5 0.2 broadcast_in_dim.4
  9.7 1.5 scatter_fusion
  11.2 19.9 %all_to_all.5 = bf16[2,32,3072]{2,0,1:T(2,128)(2,1)} all-to-all(bf16[2,32,3072]{2,0,1:T(2,128)(2,1)S(1)} %scatter_fusion), channel_id=1, replica_groups=mesh['off'=16,'img'=32] {'off'}, dimensions={1} | all-to-all | bytes 786432 | tf_op jit(solution)/shard_map/all_to_all | solution.py:49
  31.2 0.0 all-gather.2.cloned.1.call-update
  31.2 0.7 compare_select_fusion
  31.9 0.1 copy.12
  32.0 180.9 %all-gather.2.cloned.1.call-done = bf16[2,1024,3072]{2,0,1:T(2,128)(2,1)} async-done(((bf16[2,32,3072]{2,0,1:T(2,128)(2,1)}), bf16[2,1024,3072]{2,0,1:T(2,128)(2,1)}) %all-gather.2.cloned.1.call-update) | async-done | bytes 12582928 | tf_op jit(solution)/shard_map/all_gather | solution.py:52
  212.9 12.6 %copy.11 = bf16[2,1024,3072]{2,1,0:T(8,128)(2,1)} copy(bf16[2,1024,3072]{2,0,1:T(2,128)(2,1)} %all-gather.2.cloned.1.call-done) | data formatting | bytes 25165824
  225.5 28.1 %while.1 = (s32[]{:T(128)}, bf16[2,1024,3072]{2,1,0:T(8,128)(2,1)}, s32[4,3]{1,0:T(4,128)S(1)}, bf16[4,1,1024,1536]{3,2,1,0:T(8,128)(2,1)}, s32[]{:T(128)}) while((s32[]{:T(128)}, bf16[2,1024,3072]{2,1,0:T(8,128)(2,1)}, s32[4,3]{1,0:T(4,128)S(1)}, bf16[4,1,1024,1536]{3,2,1,0:T(8,128)(2,1)}, s32[]{:T(128)}) %tuple.23), condition=%wide.while_cond, body=%wide.while_body.sunk | while | flops 2 | bytes 6293097 | solution.py:29
  225.5 0.6 fusion.13
  226.1 6.4 %bitcast_dynamic-update-slice_fusion.2 = bf16[4,1,1024,1536]{3,2,1,0:T(8,128)(2,1)} fusion(bf16[4,1,1024,1536]{3,2,1,0:T(8,128)(2,1)} %get-tuple-element.72, s32[]{:T(128)} %get-tuple-element.69, bf16[2,1024,3072]{2,1,0:T(8,128)(2,1)} %get-tuple-element.75, s32[]{:T(128)} %bitcast.28, s32[]{:T(128)} %bitcast.29), kind=kLoop, calls=%fused_computation.1.clone.1 | loop fusion | bytes 6292992 | tf_op jit(solution)/shard_map/vmap()/gather
  232.5 0.6 fusion.13
  233.2 6.4 %bitcast_dynamic-update-slice_fusion.2 = bf16[4,1,1024,1536]{3,2,1,0:T(8,128)(2,1)} fusion(bf16[4,1,1024,1536]{3,2,1,0:T(8,128)(2,1)} %get-tuple-element.72, s32[]{:T(128)} %get-tuple-element.69, bf16[2,1024,3072]{2,1,0:T(8,128)(2,1)} %get-tuple-element.75, s32[]{:T(128)} %bitcast.28, s32[]{:T(128)} %bitcast.29), kind=kLoop, calls=%fused_computation.1.clone.1 | loop fusion | bytes 6292992 | tf_op jit(solution)/shard_map/vmap()/gather
  239.6 0.6 fusion.13
  240.2 6.4 %bitcast_dynamic-update-slice_fusion.2 = bf16[4,1,1024,1536]{3,2,1,0:T(8,128)(2,1)} fusion(bf16[4,1,1024,1536]{3,2,1,0:T(8,128)(2,1)} %get-tuple-element.72, s32[]{:T(128)} %get-tuple-element.69, bf16[2,1024,3072]{2,1,0:T(8,128)(2,1)} %get-tuple-element.75, s32[]{:T(128)} %bitcast.28, s32[]{:T(128)} %bitcast.29), kind=kLoop, calls=%fused_computation.1.clone.1 | loop fusion | bytes 6292992 | tf_op jit(solution)/shard_map/vmap()/gather
  246.6 0.6 fusion.13
  247.2 6.4 %bitcast_dynamic-update-slice_fusion.2 = bf16[4,1,1024,1536]{3,2,1,0:T(8,128)(2,1)} fusion(bf16[4,1,1024,1536]{3,2,1,0:T(8,128)(2,1)} %get-tuple-element.72, s32[]{:T(128)} %get-tuple-element.69, bf16[2,1024,3072]{2,1,0:T(8,128)(2,1)} %get-tuple-element.75, s32[]{:T(128)} %bitcast.28, s32[]{:T(128)} %bitcast.29), kind=kLoop, calls=%fused_computation.1.clone.1 | loop fusion | bytes 6292992 | tf_op jit(solution)/shard_map/vmap()/gather
  253.6 7.5 %fusion.2 = bf16[4,1536,128]{1,2,0:T(8,128)(2,1)} fusion(bf16[4,128,1024]{2,1,0:T(8,128)(2,1)S(1)} %bitcast.30, bf16[4,1,1024,1536]{3,2,1,0:T(8,128)(2,1)} %get-tuple-element.12), kind=kOutput, calls=%fused_computation.5 | convolution fusion | flops 1611399168 | bytes 15204352 | tf_op jit(solution)/shard_map/bcr,brt->bct/dot_general | solution.py:35
  (10 shorter events, 0.1 us)
Async XLA Ops:
  6.5 247.1 %copy-start = (bf16[1,512,1024]{2,1,0:T(8,128)(2,1)S(1)}, bf16[1,512,1024]{2,1,0:T(8,128)(2,1)}, u32[]{:S(2)}) copy-start(bf16[1,512,1024]{2,1,0:T(8,128)(2,1)} %param.9) | copy-start | bytes 3145732
  6.5 206.3 %all-gather.2.cloned.1.call-start = ((), (), s32[]{:S(2)}) async-start(), calls=%async_computation.1 | async-start | bytes 12976128 | tf_op jit(solution)/shard_map/all_gather | solution.py:52
Sparse Core Ops, SparseCore 0:
  31.3 181.5 all-gather.1
where the time goes:
time: 268 us
  waiting for transfers between devices  181 us (68%)
  local copies, waits for them, and re-layouts  43 us (16%)
  blocking collectives  19.9 us (7%)
  between operations  13.4 us (5%)
  matrix products  7.54 us (3%)
  other arithmetic  3.2 us (1%)
    all_gather x1, waiting for transfers between devices, per_device(): lax.all_gather(regrouped, 'img', axis=1, tiled=True)  181 us
    gather x12, local copies, waits for them, and re-layouts  28.1 us
    all_to_all x1, blocking collectives, per_device(): lax.all_to_all(ordered, 'off', split_axis=1, concat_axis=1, tiled=True)  19.9 us
    unnamed x4, local copies, waits for them, and re-layouts  12.7 us
    dot_general x1, matrix products, migrate_rows(): jnp.einsum('bcr,brt->bct', columns, segments, preferred_element_type=jnp....  7.54 us
  transfers between devices with their start and end apart: 1, of which 1 were waited for; matrix products, arithmetic and copies ran while one was open for 0% of the time, Pallas kernels for 0%

commit v1 on v0

--- a/solution.py
+++ b/solution.py
@@ -46,7 +46,10 @@
     initial = jnp.zeros((weight_rows.shape[0], NT), jnp.float32)
     levels = filtered_levels(traces)
     ordered = jnp.zeros_like(levels).at[:, targets].set(levels)
-    regrouped = lax.all_to_all(ordered, "off", split_axis=1, concat_axis=1, tiled=True)
+    regrouped = jnp.concatenate(
+        lax.all_to_all(jnp.stack(jnp.split(ordered, lax.axis_size("off"), axis=1)), "off", 0, 0),
+        axis=1,
+    )
     summed = migrate_rows(
         initial,
         lax.all_gather(regrouped, "img", axis=1, tiled=True),

time: 268 us -> 257 us (0.959)
  the two profiles are of different devices: /device:TPU:5 before, /device:TPU:3 now
where the time goes in v1:
time: 257 us
  waiting for transfers between devices  181 us (70%)
  local copies, waits for them, and re-layouts  31.5 us (12%)
  blocking collectives  19.8 us (8%)
  between operations  13.5 us (5%)
  matrix products  7.54 us (3%)
  other arithmetic  3.2 us (1%)
    all_gather x1, waiting for transfers between devices, per_device(): lax.all_gather(regrouped, 'img', axis=1, tiled=True)  181 us
    gather x12, local copies, waits for them, and re-layouts  28 us
    all_to_all x1, blocking collectives, per_device(): lax.all_to_all(jnp.stack(jnp.split(ordered, lax.axis_size('off'), axis=1)...  19.8 us
    dot_general x1, matrix products, migrate_rows(): jnp.einsum('bcr,brt->bct', columns, segments, preferred_element_type=jnp....  7.54 us
  transfers between devices with their start and end apart: 1, of which 1 were waited for; matrix products, arithmetic and copies ran while one was open for 0% of the time, Pallas kernels for 0%

profile of v1, /device:TPU:3, one launch (start us, length us, event | category | flops | bytes accessed | tf_op | source)
XLA Modules:
  0.0 256.6 jit_solution(16643066821547088890)
XLA Ops:
  6.5 0.0 copy-start
  6.5 1.0 convert_element_type.24
  7.6 0.3 convert_bitcast_fusion
  7.9 0.5 fusion.8
  8.4 0.4 copy.7
  8.8 0.7 compare_select_fusion.2
  9.5 0.2 broadcast_in_dim.4
  9.7 1.5 scatter_fusion
  11.7 19.8 %all_to_all.5 = bf16[16,2,2,3072]{3,1,2,0:T(2,128)(2,1)S(1)} all-to-all(bf16[16,2,2,3072]{3,1,2,0:T(2,128)(2,1)S(1)} %constant_dynamic-update-slice_fusion), channel_id=1, replica_groups=mesh['off'=16,'img'=32] {'off'}, dimensions={0} | all-to-all | bytes 786432 | tf_op jit(solution)/shard_map/all_to_all | solution.py:50
  31.6 0.8 copy.8
  32.4 0.0 all-gather.2.cloned.1.call-update
  32.4 0.7 compare_select_fusion
  33.1 0.1 copy.9
  33.2 181.0 %all-gather.2.cloned.1.call-done = bf16[2,1024,3072]{2,1,0:T(8,128)(2,1)} async-done(((bf16[2,32,3072]{2,1,0:T(8,128)(2,1)}), bf16[2,1024,3072]{2,1,0:T(8,128)(2,1)}) %all-gather.2.cloned.1.call-update) | async-done | bytes 12582928 | tf_op jit(solution)/shard_map/all_gather | solution.py:55
  214.2 28.0 %while.1 = (s32[]{:T(128)}, bf16[2,1024,3072]{2,1,0:T(8,128)(2,1)}, s32[4,3]{1,0:T(4,128)S(1)}, bf16[4,1,1024,1536]{3,2,1,0:T(8,128)(2,1)}, s32[]{:T(128)}) while((s32[]{:T(128)}, bf16[2,1024,3072]{2,1,0:T(8,128)(2,1)}, s32[4,3]{1,0:T(4,128)S(1)}, bf16[4,1,1024,1536]{3,2,1,0:T(8,128)(2,1)}, s32[]{:T(128)}) %tuple.22), condition=%wide.while_cond, body=%wide.while_body.sunk | while | flops 2 | bytes 6293097 | solution.py:29
  214.2 0.6 fusion.13
  214.8 6.4 %bitcast_dynamic-update-slice_fusion.2 = bf16[4,1,1024,1536]{3,2,1,0:T(8,128)(2,1)} fusion(bf16[4,1,1024,1536]{3,2,1,0:T(8,128)(2,1)} %get-tuple-element.68, s32[]{:T(128)} %get-tuple-element.65, bf16[2,1024,3072]{2,1,0:T(8,128)(2,1)} %get-tuple-element.71, s32[]{:T(128)} %bitcast.95, s32[]{:T(128)} %bitcast.96), kind=kLoop, calls=%fused_computation.1.clone.1 | loop fusion | bytes 6292992 | tf_op jit(solution)/shard_map/vmap()/gather
  221.2 0.6 fusion.13
  221.8 6.4 %bitcast_dynamic-update-slice_fusion.2 = bf16[4,1,1024,1536]{3,2,1,0:T(8,128)(2,1)} fusion(bf16[4,1,1024,1536]{3,2,1,0:T(8,128)(2,1)} %get-tuple-element.68, s32[]{:T(128)} %get-tuple-element.65, bf16[2,1024,3072]{2,1,0:T(8,128)(2,1)} %get-tuple-element.71, s32[]{:T(128)} %bitcast.95, s32[]{:T(128)} %bitcast.96), kind=kLoop, calls=%fused_computation.1.clone.1 | loop fusion | bytes 6292992 | tf_op jit(solution)/shard_map/vmap()/gather
  228.2 0.6 fusion.13
  228.8 6.4 %bitcast_dynamic-update-slice_fusion.2 = bf16[4,1,1024,1536]{3,2,1,0:T(8,128)(2,1)} fusion(bf16[4,1,1024,1536]{3,2,1,0:T(8,128)(2,1)} %get-tuple-element.68, s32[]{:T(128)} %get-tuple-element.65, bf16[2,1024,3072]{2,1,0:T(8,128)(2,1)} %get-tuple-element.71, s32[]{:T(128)} %bitcast.95, s32[]{:T(128)} %bitcast.96), kind=kLoop, calls=%fused_computation.1.clone.1 | loop fusion | bytes 6292992 | tf_op jit(solution)/shard_map/vmap()/gather
  235.2 0.6 fusion.13
  235.8 6.4 %bitcast_dynamic-update-slice_fusion.2 = bf16[4,1,1024,1536]{3,2,1,0:T(8,128)(2,1)} fusion(bf16[4,1,1024,1536]{3,2,1,0:T(8,128)(2,1)} %get-tuple-element.68, s32[]{:T(128)} %get-tuple-element.65, bf16[2,1024,3072]{2,1,0:T(8,128)(2,1)} %get-tuple-element.71, s32[]{:T(128)} %bitcast.95, s32[]{:T(128)} %bitcast.96), kind=kLoop, calls=%fused_computation.1.clone.1 | loop fusion | bytes 6292992 | tf_op jit(solution)/shard_map/vmap()/gather
  242.2 7.5 %fusion.2 = bf16[4,1536,128]{1,2,0:T(8,128)(2,1)} fusion(bf16[4,128,1024]{2,1,0:T(8,128)(2,1)S(1)} %bitcast.97, bf16[4,1,1024,1536]{3,2,1,0:T(8,128)(2,1)} %get-tuple-element.12), kind=kOutput, calls=%fused_computation.5 | convolution fusion | flops 1611399168 | bytes 15204352 | tf_op jit(solution)/shard_map/bcr,brt->bct/dot_general | solution.py:35
  (26 shorter events, 0.5 us)
Async XLA Ops:
  6.5 235.7 %copy-start = (bf16[1,512,1024]{2,1,0:T(8,128)(2,1)S(1)}, bf16[1,512,1024]{2,1,0:T(8,128)(2,1)}, u32[]{:S(2)}) copy-start(bf16[1,512,1024]{2,1,0:T(8,128)(2,1)} %param.9) | copy-start | bytes 3145732
  6.5 207.7 %all-gather.2.cloned.1.call-start = ((), (), s32[]{:S(2)}) async-start(), calls=%async_computation.1 | async-start | bytes 12976128 | tf_op jit(solution)/shard_map/all_gather | solution.py:55
Sparse Core Ops, SparseCore 0:
  32.5 181.6 all-gather.1

commit v2 on v0

--- a/solution.py
+++ b/solution.py
@@ -49,7 +49,9 @@
     regrouped = lax.all_to_all(ordered, "off", split_axis=1, concat_axis=1, tiled=True)
     summed = migrate_rows(
         initial,
-        lax.all_gather(regrouped, "img", axis=1, tiled=True),
+        jnp.concatenate(
+            lax.all_to_all(jnp.stack([regrouped] * lax.axis_size("img")), "img", 0, 0), axis=1
+        ),
         weight_rows,
         band_rows,
         smooth_rows,

time: 268 us -> 651 us (2.43)
  the two profiles are of different devices: /device:TPU:5 before, /device:TPU:474 now
where the time goes in v2:
time: 651 us; the launch traced here: 650 us
  waiting for transfers between devices  564 us (87%)
  local copies, waits for them, and re-layouts  47.7 us (7%)
  blocking collectives  15.5 us (2%)
  starting transfers between devices  13 us (2%)
  matrix products  7.54 us (1%)
    all_to_all x1, waiting for transfers between devices, per_device(): lax.all_to_all(jnp.stack([regrouped] * lax.axis_size('img')), 'img', 0, 0)  564 us
    gather x12, local copies, waits for them, and re-layouts  28.3 us
    all_to_all x1, blocking collectives, per_device(): lax.all_to_all(ordered, 'off', split_axis=1, concat_axis=1, tiled=True)  15.5 us
  transfers between devices with their start and end apart: 1, of which 1 were waited for; matrix products, arithmetic and copies ran while one was open for 0% of the time, Pallas kernels for 0%

profile of v2, /device:TPU:474, one launch (start us, length us, event | category | flops | bytes accessed | tf_op | source)
XLA Modules:
  0.0 650.3 jit_solution(17077278491732739575)
XLA Ops:
  0.0 1.0 convert_element_type.24
  1.0 0.3 convert_bitcast_fusion
  1.3 0.5 fusion.8
  1.8 0.4 copy.13
  2.3 0.7 compare_select_fusion.2
  2.9 0.2 broadcast_in_dim.4
  3.2 1.5 scatter_fusion
  4.7 15.5 %all_to_all.10 = bf16[2,32,3072]{2,0,1:T(2,128)(2,1)S(1)} all-to-all(bf16[2,32,3072]{2,0,1:T(2,128)(2,1)S(1)} %scatter_fusion), channel_id=1, replica_groups=mesh['off'=16,'img'=32] {'off'}, dimensions={1} | all-to-all | bytes 786432 | tf_op jit(solution)/shard_map/all_to_all | solution.py:49
  20.2 0.1 copy.14
  20.3 6.1 stack.14
  26.4 13.0 %all-to-all-start.1 = ((bf16[32,2,32,3072]{3,2,1,0:T(8,128)(2,1)}), bf16[32,2,32,3072]{3,2,1,0:T(8,128)(2,1)}, u32[]{:S(2)}, u32[]{:S(2)}) async-start(bf16[32,2,32,3072]{3,2,1,0:T(8,128)(2,1)} %stack.14), calls=%async_computation.1 | async-start | bytes 25165824 | tf_op jit(solution)/shard_map/all_to_all | solution.py:53
  39.5 0.1 copy.16
  39.6 564.0 %all-to-all-done.1 = bf16[32,2,32,3072]{3,2,1,0:T(8,128)(2,1)} async-done(((bf16[32,2,32,3072]{3,2,1,0:T(8,128)(2,1)}), bf16[32,2,32,3072]{3,2,1,0:T(8,128)(2,1)}, u32[]{:S(2)}, u32[]{:S(2)}) %all-to-all-start.1) | async-done | bytes 12582944 | tf_op jit(solution)/shard_map/all_to_all | solution.py:53
  603.6 10.9 %copy.15 = bf16[32,2,32,3072]{3,2,0,1:T(8,128)(2,1)} copy(bf16[32,2,32,3072]{3,2,1,0:T(8,128)(2,1)} %all-to-all-done.1) | data formatting | bytes 25165824 | tf_op jit(solution)/shard_map/all_to_all | solution.py:53
  614.4 28.4 %while.1 = (s32[]{:T(128)}, bf16[2,1024,3072]{2,1,0:T(8,128)(2,1)}, s32[4,3]{1,0:T(4,128)S(1)}, bf16[4,1,1024,1536]{3,2,1,0:T(8,128)(2,1)}, s32[]{:T(128)}) while((s32[]{:T(128)}, bf16[2,1024,3072]{2,1,0:T(8,128)(2,1)}, s32[4,3]{1,0:T(4,128)S(1)}, bf16[4,1,1024,1536]{3,2,1,0:T(8,128)(2,1)}, s32[]{:T(128)}) %tuple.27), condition=%wide.while_cond, body=%wide.while_body.sunk | while | flops 2 | bytes 6293097 | solution.py:29
  614.5 0.6 fusion.13
  615.1 6.4 bitcast_dynamic-update-slice_fusion.2
  621.5 0.6 fusion.13
  622.2 6.4 bitcast_dynamic-update-slice_fusion.2
  628.6 0.6 fusion.13
  629.3 6.4 bitcast_dynamic-update-slice_fusion.2
  635.7 0.6 fusion.13
  636.3 6.5 bitcast_dynamic-update-slice_fusion.2
  642.8 7.5 %fusion.2 = bf16[4,1536,128]{1,2,0:T(8,128)(2,1)} fusion(bf16[4,128,1024]{2,1,0:T(8,128)(2,1)S(1)} %bitcast.33, bf16[4,1,1024,1536]{3,2,1,0:T(8,128)(2,1)} %get-tuple-element.12), kind=kOutput, calls=%fused_computation.5 | convolution fusion | flops 1611399168 | bytes 15204352 | tf_op jit(solution)/shard_map/bcr,brt->bct/dot_general | solution.py:35
  (15 shorter events, 0.1 us)
Async XLA Ops:
  0.0 642.8 %copy-start = (bf16[1,512,1024]{2,1,0:T(8,128)(2,1)S(1)}, bf16[1,512,1024]{2,1,0:T(8,128)(2,1)}, u32[]{:S(2)}) copy-start(bf16[1,512,1024]{2,1,0:T(8,128)(2,1)} %param.9) | copy-start | bytes 3145732
  26.4 13.0 %copy-start.1 = (s32[1,4]{1,0:T(1,128)S(1)}, s32[1,4]{1,0:T(1,128)}, u32[]{:S(2)}) copy-start(s32[1,4]{1,0:T(1,128)} %param.10) | copy-start | bytes 52
  26.4 13.0 %copy-start.2 = (s32[1,4]{1,0:T(1,128)S(1)}, s32[1,4]{1,0:T(1,128)}, u32[]{:S(2)}) copy-start(s32[1,4]{1,0:T(1,128)} %param.11) | copy-start | bytes 52
  26.4 577.1 %all-to-all-start.1 = ((bf16[32,2,32,3072]{3,2,1,0:T(8,128)(2,1)}), bf16[32,2,32,3072]{3,2,1,0:T(8,128)(2,1)}, u32[]{:S(2)}, u32[]{:S(2)}) async-start(bf16[32,2,32,3072]{3,2,1,0:T(8,128)(2,1)} %stack.14), calls=%async_computation.1 | async-start | bytes 25165824 | tf_op jit(solution)/shard_map/all_to_all | solution.py:53
